TPU v7x, 256 devices: a whole 4x4x8 slice. The times are simulated.
256 devices in a mesh: narrow: 8 (over y, z_lo), wide: 8 (over z_hi, core), nys: 4 (over x).
Axes of the slice: x: 4, y: 4, z: 8 (z_hi: 4, z_lo: 2; z = z_hi * 2 + z_lo), core: 2. Of those that a mesh axis runs over, the one named last changes fastest.
Arguments:
- centers: bfloat16 [262144, 1024], P(('narrow', 'wide', 'nys')), may hold values from -6 to 6
- weights: float32 [262144, 1000], P(('narrow', 'wide', 'nys')), may hold values from -6 to 6
- batch_points: bfloat16 [512, 1024], P(('narrow', 'wide', 'nys')), may hold values from -6 to 6
- labels: float32 [512, 1000], P(('narrow', 'wide', 'nys')), may hold values from -6 to 6
- nystrom_points: bfloat16 [2048, 1024], P(('narrow', 'nys')), may hold values from -6 to 6
- eigvecs: float32 [2048, 160], P(('narrow', 'nys')), may hold values from -0.125 to 0.125
- corrections: float32 [160], replicated, may hold values from 0.05 to 0.5
Outputs:
- new_weights: float32 [262144, 1000], P(('narrow', 'wide', 'nys'))
All inputs are finite; a program needn't handle non-finite values.
Results may differ from a plain program's by a relative error of at most 0.0003.
The roundings to bfloat16 on the way count: a program that leaves them out, or rounds other values in their place, can miss the bound.
Values may be sent and summed in bfloat16 or wider, within the bound.
A program may use at most 64 MiB of HBM per device.

v0:
```python
import math
import jax
import jax.numpy as jnp
from jax import lax
from jax.sharding import PartitionSpec as P

BATCH = 512
RATE = 16.0
SPREAD = 4.0


def kernel_with(left, left_sq, right):
    cross = lax.dot_general(
        left, right, (((1,), (1,)), ((), ())), preferred_element_type=jnp.float32
    )
    right_sq = jnp.sum(jnp.square(right.astype(jnp.float32)), axis=1)
    dist = jnp.sqrt(jnp.maximum(left_sq[:, None] + right_sq[None, :] - 2.0 * cross, 0.0))
    radius = math.sqrt(2.0 * left.shape[1])
    return jnp.exp((radius - dist) / SPREAD).astype(jnp.bfloat16)


def squares(points):
    return jnp.sum(jnp.square(points.astype(jnp.float32)), axis=1)


def per_device(centers, weights, batch_points, labels, nystrom_points, eigvecs, corrections):
    batch_all = lax.all_gather(batch_points, ("narrow", "wide", "nys"), axis=0, tiled=True)
    count = lax.axis_size(("narrow", "wide", "nys"))
    scale = (centers.shape[0] * count) ** (-0.5)
    center_sq = squares(centers)
    k_batch = kernel_with(centers, center_sq, batch_all)
    partial_value = (
        lax.dot_general(
            k_batch,
            weights.astype(jnp.bfloat16),
            (((0,), (0,)), ((), ())),
            preferred_element_type=jnp.float32,
        )
        * scale
    )
    rows = labels.shape[0]
    offset = lax.axis_index(("narrow", "wide", "nys")) * rows
    placed = lax.dynamic_update_slice(jnp.zeros_like(partial_value), labels, (offset, jnp.int32(0)))
    residual = lax.psum(partial_value - placed, ("narrow", "wide", "nys")).astype(jnp.bfloat16)
    k_nystrom = kernel_with(nystrom_points, squares(nystrom_points), batch_all)
    pulled = jnp.dot(k_nystrom, residual, preferred_element_type=jnp.float32)
    local_proj = lax.dot_general(
        eigvecs, pulled, (((0,), (0,)), ((), ())), precision=lax.Precision.HIGHEST
    )
    projected = lax.psum(local_proj, ("narrow", "nys"))
    scaled_proj = corrections[:, None] * projected
    gradient = jnp.dot(k_batch, residual, preferred_element_type=jnp.float32)
    corrected = jnp.dot(eigvecs, scaled_proj, precision=lax.Precision.HIGHEST).astype(jnp.bfloat16)
    points = lax.all_gather(nystrom_points, ("narrow", "nys"), axis=0, tiled=True)
    coefs = lax.all_gather(corrected, ("narrow", "nys"), axis=0, tiled=True)
    tile = kernel_with(centers, center_sq, points)
    nystrom_term = jnp.dot(tile, coefs, preferred_element_type=jnp.float32)
    return weights - RATE / BATCH * (gradient - nystrom_term)


def solution(mesh):
    placed = (
        P(("narrow", "wide", "nys"), None),
        P(("narrow", "wide", "nys"), None),
        P(("narrow", "wide", "nys"), None),
        P(("narrow", "wide", "nys"), None),
        P(("narrow", "nys"), None),
        P(("narrow", "nys"), None),
        P(),
    )
    return jax.shard_map(
        per_device,
        mesh=mesh,
        in_specs=placed,
        out_specs=P(("narrow", "wide", "nys"), None),
        check_vma=False,
    )
```

profile of v0, /device:TPU:2, one launch (start us, length us, event | category | flops | bytes accessed | tf_op | source)
XLA Modules:
  0.0 1286.6 jit_solution(18334620316952581570)
XLA Ops:
  6.5 0.0 copy-start
  6.5 0.0 all-gather.9.cloned.1.call-start
  6.5 0.7 all-gather.9.cloned.1.call-update
  7.3 0.0 all-reduce.3.cloned.1.call-start
  7.3 0.9 copy.9
  8.2 0.2 broadcast_in_dim.2
  8.5 6.3 dynamic_update_slice.3
  14.8 1.0 multiply_reduce_fusion.3
  15.8 2.1 multiply_reduce_fusion.1
  17.9 523.6 %all-gather.9.cloned.1.call-done = bf16[256,2,1024]{2,1,0:T(2,128)(2,1)} async-done(((bf16[1,2,1024]{2,1,0:T(2,128)(2,1)}), bf16[256,2,1024]{2,1,0:T(2,128)(2,1)}) %all-gather.9.cloned.1.call-update) | async-done | bytes 1048592 | tf_op jit(solution)/shard_map/all_gather | solution.py:27
  541.5 1.5 reshape.6
  543.0 0.3 multiply_reduce_fusion.2
  543.3 0.0 copy-start.1
  543.3 3.8 exponential_convert_fusion.1
  547.1 0.0 copy-start.2
  547.1 1.1 copy-done.2
  548.2 0.0 copy-done.1
  548.2 0.0 copy-start.4
  548.2 2.6 multiply_subtract_fusion.1
  550.7 0.0 copy-start.5
  550.7 81.6 %all-reduce.4 = bf16[512,1000]{0,1:T(8,128)(2,1)S(1)} all-reduce(f32[512,1000]{0,1:T(8,128)} %multiply_subtract_fusion.1), channel_id=1, replica_groups=mesh['narrow'=8,'wide'=8,'nys'=4] {'narrow','wide','nys'}, use_global_device_ids=true, to_apply=%region_2.0 | all-reduce | flops 512000 | bytes 3072000 | tf_op jit(solution)/shard_map/psum | solution.py:44
  632.3 0.0 copy-done.4
  632.3 0.8 fusion.12
  633.2 0.0 copy-done
  633.2 1.6 convolution_bitcast_fusion
  634.7 0.0 all-reduce.3.cloned.1.call-update
  634.7 0.0 all-gather.5.cloned.1.call-start
  634.8 0.7 all-gather.5.cloned.1.call-update
  635.5 0.2 all-gather.7.cloned.1.call-start
  635.7 301.3 %all-reduce.3.cloned.1.call-done = f32[160,1000]{1,0:T(8,128)} async-done(((f32[160,1000]{1,0:T(8,128)}), f32[160,1000]{1,0:T(8,128)}) %all-reduce.3.cloned.1.call-update) | async-done | bytes 640016 | tf_op jit(solution)/shard_map/psum | solution.py:50
  937.0 0.0 copy-done.5
  937.0 2.3 fusion.4
  939.4 0.0 all-gather.7.cloned.1.call-update
  939.4 157.5 %all-gather.5.cloned.1.call-done = bf16[2048,1024]{1,0:T(8,128)(2,1)} async-done(((bf16[64,1024]{1,0:T(8,128)(2,1)}), bf16[2048,1024]{1,0:T(8,128)(2,1)}) %all-gather.5.cloned.1.call-update) | async-done | bytes 4194320 | tf_op jit(solution)/shard_map/all_gather | solution.py:54
  1097.0 3.1 multiply_reduce_fusion
  1100.0 0.0 copy-start.3
  1100.1 157.9 %all-gather.7.cloned.1.call-done = bf16[2048,1000]{1,0:T(8,128)(2,1)} async-done(((bf16[64,1000]{1,0:T(8,128)(2,1)}), bf16[2048,1000]{1,0:T(8,128)(2,1)}) %all-gather.7.cloned.1.call-update) | async-done | bytes 4096016 | tf_op jit(solution)/shard_map/all_gather | solution.py:55
  1258.0 15.5 %fusion.13 = f32[1024,1000]{0,1:T(8,128)} fusion(bf16[2048,1000]{1,0:T(8,128)(2,1)} %all-gather.7.cloned.1.call-done, bf16[1024,1024]{1,0:T(8,128)(2,1)} %param.7, bf16[2048,1024]{1,0:T(8,128)(2,1)} %all-gather.5.cloned.1.call-done, f32[2048]{0:T(1024)S(1)} %multiply_reduce_fusion, f32[1024]{0:T(1024)S(1)} %multiply_reduce_fusion.1), kind=kOutput, calls=%fused_computation.21 | convolution fusion | flops 8503951360 | bytes 14495744 | tf_op jit(solution)/shard_map/dot_general | solution.py:57
  1273.5 0.0 copy-done.3
  1273.5 6.7 multiply_subtract_fusion
Async XLA Ops:
  6.5 626.6 %copy-start = (f32[64,160]{1,0:T(8,128)S(1)}, f32[64,160]{1,0:T(8,128)}, u32[]{:S(2)}) copy-start(f32[64,160]{1,0:T(8,128)} %param.12) | copy-start | bytes 122884
  6.5 535.0 %all-gather.9.cloned.1.call-start = ((), (), s32[]{:S(2)}) async-start(), calls=%async_computation.3 | async-start | bytes 1052672 | tf_op jit(solution)/shard_map/all_gather | solution.py:27
  7.3 929.8 %all-reduce.3.cloned.1.call-start = ((), (), s32[]{:S(2)}) async-start(), calls=%async_computation.1 | async-start | bytes 1310720 | tf_op jit(solution)/shard_map/psum | solution.py:50
  543.3 4.9 copy-start.1
  547.1 1.1 copy-start.2
  548.2 84.1 %copy-start.4 = (bf16[64,1024]{1,0:T(8,128)(2,1)S(1)}, bf16[64,1024]{1,0:T(8,128)(2,1)}, u32[]{:S(2)}) copy-start(bf16[64,1024]{1,0:T(8,128)(2,1)} %param.11) | copy-start | bytes 393220
  550.7 386.3 %copy-start.5 = (f32[160]{0:T(256)S(1)}, f32[160]{0:T(256)}, u32[]{:S(2)}) copy-start(f32[160]{0:T(256)} %param.13) | copy-start | bytes 1924
  634.7 462.2 %all-gather.5.cloned.1.call-start = ((), (), s32[]{:S(2)}) async-start(), calls=%async_computation | async-start | bytes 4325376 | tf_op jit(solution)/shard_map/all_gather | solution.py:54
  635.5 622.5 %all-gather.7.cloned.1.call-start = ((), (), s32[]{:S(2)}) async-start(), calls=%async_computation.2 | async-start | bytes 4325376 | tf_op jit(solution)/shard_map/all_gather | solution.py:55
  1100.0 173.4 %copy-start.3 = (bf16[1024,512]{1,0:T(8,128)(2,1)S(1)}, bf16[1024,512]{1,0:T(8,128)(2,1)}, u32[]{:S(2)}) copy-start(bf16[1024,512]{1,0:T(8,128)(2,1)} %copy-done.2) | copy-start | bytes 3145732
Sparse Core Ops, SparseCore 0:
  9.2 532.3 all-gather.8
  634.9 302.1 all-reduce.2
  939.0 157.9 all-gather.4
  1098.7 159.1 all-gather.6
where the time goes:
time: 1290 us
  waiting for transfers between devices  1140 us (88%)
  blocking collectives  81.6 us (6%)
  matrix products  33.3 us (3%)
  between operations  13.2 us (1%)
    all_gather x1, waiting for transfers between devices, per_device(): lax.all_gather(batch_points, ('narrow', 'wide', 'nys'), axis=0, tiled=True)  524 us
    psum x1, waiting for transfers between devices, per_device(): projected = lax.psum(local_proj, ('narrow', 'nys'))  301 us
    all_gather x1, waiting for transfers between devices, per_device(): coefs = lax.all_gather(corrected, ('narrow', 'nys'), axis=0, tiled=True)  158 us
    all_gather x1, waiting for transfers between devices, per_device(): lax.all_gather(nystrom_points, ('narrow', 'nys'), axis=0, tiled=True)  158 us
    psum x1, blocking collectives, per_device(): lax.psum(partial_value - placed, ('narrow', 'wide', 'nys'))  81.6 us
  transfers between devices with their start and end apart: 4, of which 4 were waited for; matrix products, arithmetic and copies ran while one was open for 1% of the time, Pallas kernels for 0%

commit v1 on v0

--- a/solution.py
+++ b/solution.py
@@ -47,7 +47,7 @@
     local_proj = lax.dot_general(
         eigvecs, pulled, (((0,), (0,)), ((), ())), precision=lax.Precision.HIGHEST
     )
-    projected = lax.psum(local_proj, ("narrow", "nys"))
+    projected = lax.psum(lax.psum(local_proj, "nys"), "narrow")
     scaled_proj = corrections[:, None] * projected
     gradient = jnp.dot(k_batch, residual, preferred_element_type=jnp.float32)
     corrected = jnp.dot(eigvecs, scaled_proj, precision=lax.Precision.HIGHEST).astype(jnp.bfloat16)

time: 1290 us -> 1040 us (0.81)
  waiting for transfers between devices: 1140 us -> 893 us
    psum x1 -> x2, waiting for transfers between devices: 301 us -> 134 us  [per_device(): projected = lax.psum(lax.psum(local_proj, 'nys'), 'narrow')]
    all_gather x1, waiting for transfers between devices: 158 us -> 76.2 us  [per_device(): lax.all_gather(nystrom_points, ('narrow', 'nys'), axis=0, tiled=True)]
  transfers between devices with their start and end apart: 4 -> 5, of which waited for: 4 -> 5; matrix products, arithmetic and copies ran while one was open for 1% -> 2% of each run, Pallas kernels for 0% -> 0%
where the time goes in v1:
time: 1040 us
  waiting for transfers between devices  893 us (86%)
  blocking collectives  81.6 us (8%)
  matrix products  33.3 us (3%)
  between operations  14.7 us (1%)
    all_gather x1, waiting for transfers between devices, per_device(): lax.all_gather(batch_points, ('narrow', 'wide', 'nys'), axis=0, tiled=True)  524 us
    all_gather x1, waiting for transfers between devices, per_device(): coefs = lax.all_gather(corrected, ('narrow', 'nys'), axis=0, tiled=True)  158 us
    psum x2, waiting for transfers between devices, per_device(): projected = lax.psum(lax.psum(local_proj, 'nys'), 'narrow')  134 us
    psum x1, blocking collectives, per_device(): lax.psum(partial_value - placed, ('narrow', 'wide', 'nys'))  81.6 us
    all_gather x1, waiting for transfers between devices, per_device(): lax.all_gather(nystrom_points, ('narrow', 'nys'), axis=0, tiled=True)  76.2 us
  transfers between devices with their start and end apart: 5, of which 5 were waited for; matrix products, arithmetic and copies ran while one was open for 2% of the time, Pallas kernels for 0%

profile of v1, /device:TPU:2, one launch (start us, length us, event | category | flops | bytes accessed | tf_op | source)
XLA Modules:
  0.0 1038.8 jit_solution(12629331509632987009)
XLA Ops:
  7.4 0.0 copy-start
  7.4 0.0 all-gather.9.cloned.1.call-start
  7.4 0.7 all-gather.9.cloned.1.call-update
  8.1 0.0 all-reduce.4.cloned.1.call-start
  8.1 0.9 copy.9
  9.1 0.2 broadcast_in_dim.2
  9.3 6.3 dynamic_update_slice.3
  15.6 1.0 multiply_reduce_fusion.3
  16.6 2.1 multiply_reduce_fusion.1
  18.7 523.6 %all-gather.9.cloned.1.call-done = bf16[256,2,1024]{2,1,0:T(2,128)(2,1)} async-done(((bf16[1,2,1024]{2,1,0:T(2,128)(2,1)}), bf16[256,2,1024]{2,1,0:T(2,128)(2,1)}) %all-gather.9.cloned.1.call-update) | async-done | bytes 1048592 | tf_op jit(solution)/shard_map/all_gather | solution.py:27
  542.3 1.5 reshape.6
  543.8 0.3 multiply_reduce_fusion.2
  544.1 0.0 copy-start.1
  544.1 3.8 exponential_convert_fusion.1
  547.9 0.0 copy-start.2
  547.9 1.1 copy-done.2
  549.0 0.0 copy-done.1
  549.0 0.0 copy-start.4
  549.0 2.6 multiply_subtract_fusion.1
  551.6 0.0 copy-start.5
  551.6 81.6 %all-reduce.7 = bf16[512,1000]{0,1:T(8,128)(2,1)S(1)} all-reduce(f32[512,1000]{0,1:T(8,128)} %multiply_subtract_fusion.1), channel_id=1, replica_groups=mesh['narrow'=8,'wide'=8,'nys'=4] {'narrow','wide','nys'}, use_global_device_ids=true, to_apply=%region_2.0 | all-reduce | flops 512000 | bytes 3072000 | tf_op jit(solution)/shard_map/psum | solution.py:44
  633.1 0.0 copy-done.4
  633.1 0.8 fusion.12
  634.0 0.0 copy-done
  634.0 1.6 convolution_bitcast_fusion
  635.5 0.0 all-reduce.4.cloned.1.call-update
  635.6 0.0 all-reduce.6.cloned.1.call-start
  635.6 46.4 %all-reduce.4.cloned.1.call-done = f32[160,1000]{1,0:T(8,128)} async-done(((f32[160,1000]{1,0:T(8,128)}), f32[160,1000]{1,0:T(8,128)}) %all-reduce.4.cloned.1.call-update) | async-done | bytes 640016 | tf_op jit(solution)/shard_map/psum | solution.py:50
  682.0 0.0 all-reduce.6.cloned.1.call-update
  682.0 0.0 all-gather.5.cloned.1.call-start
  682.1 0.5 all-gather.5.cloned.1.call-update
  682.6 0.2 all-gather.7.cloned.1.call-start
  682.8 87.5 %all-reduce.6.cloned.1.call-done = f32[160,1000]{1,0:T(8,128)} async-done(((f32[160,1000]{1,0:T(8,128)}), f32[160,1000]{1,0:T(8,128)}) %all-reduce.6.cloned.1.call-update) | async-done | bytes 640016 | tf_op jit(solution)/shard_map/psum | solution.py:50
  770.3 0.0 copy-done.5
  770.3 2.3 fusion.4
  772.7 0.0 all-gather.7.cloned.1.call-update
  772.7 76.2 %all-gather.5.cloned.1.call-done = bf16[2048,1024]{1,0:T(8,128)(2,1)} async-done(((bf16[64,1024]{1,0:T(8,128)(2,1)}), bf16[2048,1024]{1,0:T(8,128)(2,1)}) %all-gather.5.cloned.1.call-update) | async-done | bytes 4194320 | tf_op jit(solution)/shard_map/all_gather | solution.py:54
  848.9 3.1 multiply_reduce_fusion
  852.0 0.0 copy-start.3
  852.0 157.6 %all-gather.7.cloned.1.call-done = bf16[2048,1000]{1,0:T(8,128)(2,1)} async-done(((bf16[64,1000]{1,0:T(8,128)(2,1)}), bf16[2048,1000]{1,0:T(8,128)(2,1)}) %all-gather.7.cloned.1.call-update) | async-done | bytes 4096016 | tf_op jit(solution)/shard_map/all_gather | solution.py:55
  1009.6 15.5 %fusion.13 = f32[1024,1000]{0,1:T(8,128)} fusion(bf16[2048,1000]{1,0:T(8,128)(2,1)} %all-gather.7.cloned.1.call-done, bf16[1024,1024]{1,0:T(8,128)(2,1)} %param.7, bf16[2048,1024]{1,0:T(8,128)(2,1)} %all-gather.5.cloned.1.call-done, f32[2048]{0:T(1024)S(1)} %multiply_reduce_fusion, f32[1024]{0:T(1024)S(1)} %multiply_reduce_fusion.1), kind=kOutput, calls=%fused_computation.21 | convolution fusion | flops 8503951360 | bytes 14495744 | tf_op jit(solution)/shard_map/dot_general | solution.py:57
  1025.1 0.0 copy-done.3
  1025.1 6.7 multiply_subtract_fusion
Async XLA Ops:
  7.4 626.6 %copy-start = (f32[64,160]{1,0:T(8,128)S(1)}, f32[64,160]{1,0:T(8,128)}, u32[]{:S(2)}) copy-start(f32[64,160]{1,0:T(8,128)} %param.12) | copy-start | bytes 122884
  7.4 535.0 %all-gather.9.cloned.1.call-start = ((), (), s32[]{:S(2)}) async-start(), calls=%async_computation.4 | async-start | bytes 1052672 | tf_op jit(solution)/shard_map/all_gather | solution.py:27
  8.1 673.9 %all-reduce.4.cloned.1.call-start = ((), (), s32[]{:S(2)}) async-start(), calls=%async_computation.1 | async-start | bytes 1310720 | tf_op jit(solution)/shard_map/psum | solution.py:50
  544.1 4.9 copy-start.1
  547.9 1.1 copy-start.2
  549.0 84.1 %copy-start.4 = (bf16[64,1024]{1,0:T(8,128)(2,1)S(1)}, bf16[64,1024]{1,0:T(8,128)(2,1)}, u32[]{:S(2)}) copy-start(bf16[64,1024]{1,0:T(8,128)(2,1)} %param.11) | copy-start | bytes 393220
  551.6 218.8 %copy-start.5 = (f32[160]{0:T(256)S(1)}, f32[160]{0:T(256)}, u32[]{:S(2)}) copy-start(f32[160]{0:T(256)} %param.13) | copy-start | bytes 1924
  635.6 134.8 %all-reduce.6.cloned.1.call-start = ((), (), s32[]{:S(2)}) async-start(), calls=%async_computation.2 | async-start | bytes 1310720 | tf_op jit(solution)/shard_map/psum | solution.py:50
  682.0 166.9 %all-gather.5.cloned.1.call-start = ((), (), s32[]{:S(2)}) async-start(), calls=%async_computation | async-start | bytes 4325376 | tf_op jit(solution)/shard_map/all_gather | solution.py:54
  682.6 327.0 %all-gather.7.cloned.1.call-start = ((), (), s32[]{:S(2)}) async-start(), calls=%async_computation.3 | async-start | bytes 4325376 | tf_op jit(solution)/shard_map/all_gather | solution.py:55
  852.0 173.1 %copy-start.3 = (bf16[1024,512]{1,0:T(8,128)(2,1)S(1)}, bf16[1024,512]{1,0:T(8,128)(2,1)}, u32[]{:S(2)}) copy-start(bf16[1024,512]{1,0:T(8,128)(2,1)} %copy-done.2) | copy-start | bytes 3145732
Sparse Core Ops, SparseCore 0:
  10.0 532.3 all-gather.8
  635.7 46.2 all-reduce.3
  684.6 85.6 all-reduce.5
Sparse Core Ops, SparseCore 1:
  684.3 164.6 all-gather.4
  850.6 158.9 all-gather.6
